TPU v7x, 32 devices: a whole 2x2x4 slice. The times are simulated.
32 devices in a mesh: groups: 2 (over y), member: 2 (over core), fsdp: 8 (over z, x).
Axes of the slice: x: 2, y: 2, z: 4, core: 2. Of those that a mesh axis runs over, the one named last changes fastest.
Arguments:
- features: bfloat16 [16, 128, 4096], P(('groups', 'fsdp')), parts along dimension 0, may hold values from -6 to 6
- blocks: int32 [4, 2], P(('groups', 'member')), parts along dimension 0, may hold values from 0 to 7
- pair_labels: int32 [4, 4, 2], P(('groups', 'member')), parts along dimension 0, may hold values from 0 to 1, as said below
- ffn_gain: float32 [2, 4096], P('member'), may hold values from 0.5 to 2
- final_gain: float32 [2, 4096], P('member'), may hold values from 0.5 to 2
- score_head: float32 [2, 4096], P('member'), may hold values from -0.75 to 0.75
- w_gate: bfloat16 [2, 4096, 14336], P('member', None, 'fsdp'), may hold values from -0.09375 to 0.09375
- w_up: bfloat16 [2, 4096, 14336], P('member', None, 'fsdp'), may hold values from -1 to 1
- w_down: bfloat16 [2, 14336, 4096], P('member', 'fsdp'), may hold values from -1 to 1
Outputs:
- pair_loss: float32 [4], P(('groups', 'member')), parts along dimension 0
- grad_gate: bfloat16 [4, 4096, 14336], P(('groups', 'member'), None, 'fsdp'), parts along dimension 0
- grad_up: bfloat16 [4, 4096, 14336], P(('groups', 'member'), None, 'fsdp'), parts along dimension 0
- grad_down: bfloat16 [4, 14336, 4096], P(('groups', 'member'), 'fsdp'), parts along dimension 0
- grad_head: float32 [4, 4096], P(('groups', 'member'), 'fsdp'), parts along dimension 0
- grad_final_gain: float32 [4, 4096], P(('groups', 'member'), 'fsdp'), parts along dimension 0
- grad_ffn_gain: float32 [4, 4096], P(('groups', 'member'), 'fsdp'), parts along dimension 0
- grad_features: bfloat16 [16, 128, 4096], P(('groups', 'fsdp')), parts along dimension 0
There are 2 independent parts, one for each index of `groups`. A program takes and returns all parts, laid end to end along the dimension named above; an argument that names none is the same for every part. Nothing has to cross between parts.
Inputs may be any that keep to these rules, and one draw needn't show every extreme that they name: `pair_labels`: in every pair the chosen and the rejected entry differ.
All inputs are finite; a program needn't handle non-finite values.
Results may differ from a plain program's by a relative error of at most 0.008.
Values may be sent and summed in bfloat16 or wider, within the bound.
No kernel may reach another device: no remote copies, remote signals or barrier semaphores. Data moves between devices by JAX's collectives and lax.ppermute only.
A program may use at most 256 MiB of HBM per device.

v0:
```python
import jax
import jax.numpy as jnp
from jax import lax
from jax.sharding import PartitionSpec as P

eps = 1e-05
loss_scale = 256.0


def pair_terms(scores, pair_rows, entries, block_len):
    reward = jnp.mean(scores.reshape(entries, block_len), axis=1)
    slots = jnp.arange(entries, dtype=jnp.int32)
    select = (pair_rows[:, 0:1] == slots[None, :]).astype(jnp.float32) - (
        pair_rows[:, 1:2] == slots[None, :]
    ).astype(jnp.float32)
    margin = jnp.sum(select * reward[None, :], axis=1)
    total_loss = jnp.sum(jax.nn.softplus(-margin))
    weights = -jax.nn.sigmoid(-margin) * loss_scale
    dreward = jnp.sum(select * weights[:, None], axis=0)
    dscore = jnp.repeat(dreward / block_len, block_len, total_repeat_length=entries * block_len)
    return (total_loss, dscore)


def contract(left, right, left_dim, right_dim):
    return lax.dot_general(
        left, right, (((left_dim,), (right_dim,)), ((), ())), preferred_element_type=jnp.float32
    )


def body(features, blocks, pair_labels, ffn_gain, final_gain, score_head, w_gate, w_up, w_down):
    nodes = lax.axis_size("fsdp")
    position = lax.axis_index("fsdp")
    owned_count = features.shape[0]
    block_len = features.shape[1]
    model_width = features.shape[2]
    columns = model_width // nodes
    start = position * columns
    chosen_blocks = blocks[0]
    entries = chosen_blocks.shape[0]
    row_count = entries * block_len
    owner = chosen_blocks // owned_count
    local_index = chosen_blocks - owner * owned_count
    is_mine = owner == position
    picked = jnp.take(features, local_index, axis=0)
    outgoing = jnp.where(is_mine[:, None, None], picked, jnp.zeros_like(picked))
    arrived = lax.all_to_all(outgoing[None], "fsdp", split_axis=3, concat_axis=0, tiled=True)
    bands = jnp.sum(arrived, axis=0, dtype=jnp.float32).astype(jnp.bfloat16)
    gathered = lax.all_gather(bands, "fsdp", axis=2, tiled=True)
    inputs = gathered.reshape(row_count, model_width).astype(jnp.float32)
    inverse_in = lax.rsqrt(jnp.mean(inputs * inputs, axis=1, keepdims=True) + eps)
    normed_in = inputs * inverse_in
    scaled_in = (normed_in * ffn_gain[0][None, :]).astype(jnp.bfloat16)
    gate_pre = jnp.dot(scaled_in, w_gate[0], preferred_element_type=jnp.float32)
    up_pre = jnp.dot(scaled_in, w_up[0], preferred_element_type=jnp.float32)
    silu_gate = jax.nn.silu(gate_pre)
    hidden = (silu_gate * up_pre).astype(jnp.bfloat16)
    out_part = jnp.dot(hidden, w_down[0], preferred_element_type=jnp.float32)
    gain_head = final_gain[0] * score_head[0]
    final_share = lax.dynamic_slice_in_dim(final_gain[0], start, columns, 0)
    head_share = lax.dynamic_slice_in_dim(score_head[0], start, columns, 0)
    ffn_share = lax.dynamic_slice_in_dim(ffn_gain[0], start, columns, 0)
    normed_in_share = lax.dynamic_slice_in_dim(normed_in, start, columns, 1)
    out_total = lax.psum(out_part, "fsdp")
    summed = inputs + out_total
    inverse_out = lax.rsqrt(jnp.mean(summed * summed, axis=1, keepdims=True) + eps)
    normed_out = summed * inverse_out
    scores = jnp.sum(normed_out * gain_head[None, :], axis=1)
    total_loss, dscore = pair_terms(scores, pair_labels[0], entries, block_len)
    dsummed = inverse_out * (
        dscore[:, None] * gain_head[None, :] - normed_out * (dscore * scores / model_width)[:, None]
    )
    dsummed_b = dsummed.astype(jnp.bfloat16)
    normed_share = lax.dynamic_slice_in_dim(normed_out, start, columns, 1)
    dsummed_share = lax.dynamic_slice_in_dim(dsummed, start, columns, 1)
    weighted = jnp.sum(dscore[:, None] * normed_share, axis=0)
    grad_head = final_share * weighted
    grad_final = head_share * weighted
    grad_down = contract(hidden, dsummed_b, 0, 0).astype(jnp.bfloat16)
    dhidden = contract(dsummed_b, w_down[0], 1, 1)
    sigmoid_gate = jax.nn.sigmoid(gate_pre)
    grad_gate_pre = (
        dhidden * up_pre * sigmoid_gate * (1.0 + gate_pre * (1.0 - sigmoid_gate))
    ).astype(jnp.bfloat16)
    grad_up_pre = (dhidden * silu_gate).astype(jnp.bfloat16)
    grad_gate = contract(scaled_in, grad_gate_pre, 0, 0).astype(jnp.bfloat16)
    grad_up = contract(scaled_in, grad_up_pre, 0, 0).astype(jnp.bfloat16)
    dscaled_part = contract(grad_gate_pre, w_gate[0], 1, 1) + contract(grad_up_pre, w_up[0], 1, 1)
    dscaled_share = lax.psum_scatter(dscaled_part, "fsdp", scatter_dimension=1, tiled=True)
    grad_ffn = jnp.sum(dscaled_share * normed_in_share, axis=0)
    dnormed_share = dscaled_share * ffn_share[None, :]
    row_inner = lax.psum(jnp.sum(dnormed_share * normed_in_share, axis=1), "fsdp")
    drows_share = (
        inverse_in * (dnormed_share - normed_in_share * (row_inner / model_width)[:, None])
        + dsummed_share
    )
    drows_share = drows_share.astype(jnp.bfloat16).reshape(entries, block_len, columns)
    owners = jnp.arange(nodes, dtype=jnp.int32)
    to_owner = owner[None, :] == owners[:, None]
    outgoing_back = jnp.where(
        to_owner[:, :, None, None], drows_share[None], jnp.zeros_like(drows_share[None])
    )
    returned = lax.all_to_all(outgoing_back, "fsdp", split_axis=0, concat_axis=3, tiled=True)[0]
    owner_hit = (
        (local_index[None, :] == jnp.arange(owned_count, dtype=jnp.int32)[:, None])
        & is_mine[None, :]
    ).astype(jnp.bfloat16)
    partial_grad = jnp.einsum(
        "kl,lbd->kbd", owner_hit, returned, preferred_element_type=jnp.float32
    )
    total_grad = lax.psum(partial_grad.astype(jnp.bfloat16), "member")
    return (
        total_loss.reshape(1),
        grad_gate[None],
        grad_up[None],
        grad_down[None],
        grad_head[None],
        grad_final[None],
        grad_ffn[None],
        total_grad,
    )


def solution(mesh):
    in_specs = (
        P(("groups", "fsdp"), None, None),
        P(("groups", "member"), None),
        P(("groups", "member"), None, None),
        P("member", None),
        P("member", None),
        P("member", None),
        P("member", None, "fsdp"),
        P("member", None, "fsdp"),
        P("member", "fsdp", None),
    )
    out_specs = (
        P(("groups", "member")),
        P(("groups", "member"), None, "fsdp"),
        P(("groups", "member"), None, "fsdp"),
        P(("groups", "member"), "fsdp", None),
        P(("groups", "member"), "fsdp"),
        P(("groups", "member"), "fsdp"),
        P(("groups", "member"), "fsdp"),
        P(("groups", "fsdp"), None, None),
    )
    return jax.shard_map(body, mesh=mesh, in_specs=in_specs, out_specs=out_specs, check_vma=False)
```

profile of v0, /device:TPU:0, one launch (start us, length us, event | category | flops | bytes accessed | tf_op | source)
XLA Modules:
  0.0 576.1 jit_solution(16687666453106717526)
XLA Ops:
  7.2 0.0 all-gather.2.cloned.1.call-start
  7.2 1.6 copy.29
  8.8 0.7 broadcast_compare_fusion
  9.5 2.3 broadcast_select_fusion
  11.8 0.0 copy-start.8
  11.8 55.3 %all_to_all.27 = bf16[1,2,128,4096]{2,1,0,3:T(2,128)(2,1)S(1)} all-to-all(bf16[1,2,128,4096]{2,1,0,3:T(2,128)(2,1)S(1)} %broadcast_select_fusion), channel_id=1, replica_groups=mesh['groups'=2,'member'=2,'fsdp'=8] {'fsdp'}, dimensions={3} | all-to-all | bytes 4194304 | tf_op jit(solution)/shard_map/all_to_all | solution.py:46
  67.1 3.2 reduce_sum.104
  70.3 0.0 all-gather.2.cloned.1.call-update
  70.3 0.5 all-reduce.3.cloned.1.call-start
  70.8 48.0 %all-gather.2.cloned.1.call-done = bf16[2,128,4096]{1,0,2:T(2,128)(2,1)} async-done(((bf16[2,128,512]{1,0,2:T(2,128)(2,1)}), bf16[2,128,4096]{1,0,2:T(2,128)(2,1)}) %all-gather.2.cloned.1.call-update) | async-done | bytes 2097168 | tf_op jit(solution)/shard_map/all_gather | solution.py:48
  118.8 5.4 multiply_reduce_fusion.2
  124.2 12.9 %multiply_convert_fusion.1 = bf16[2,128,4096]{1,0,2:T(2,128)(2,1)S(1)} fusion(f32[4096]{0:T(1024)S(1)} %bitcast.107, bf16[2,128,4096]{1,0,2:T(2,128)(2,1)} %all-gather.2.cloned.1.call-done, f32[2,128]{1,0:T(2,128)S(1)} %get-tuple-element.32), kind=kLoop, calls=%fused_computation.25 | loop fusion | flops 4194304 | bytes 4211712 | tf_op jit(solution)/shard_map/convert_element_type | solution.py:52
  137.1 0.0 slice-start
  137.1 0.0 slice-start.1
  137.1 8.1 %fusion.10 = f32[256,1792]{1,0:T(8,128)S(1)} fusion(bf16[1,4096,1792]{2,1,0:T(8,128)(2,1)} %param.17, bf16[512,8,2,128]{3,2,1,0:T(2,128)(2,1)S(1)} %bitcast.101), kind=kOutput, calls=%fused_computation.13 | convolution fusion | flops 3758096384 | bytes 18612224 | tf_op jit(solution)/shard_map/dot_general | solution.py:53
  145.2 0.0 slice-start.2
  145.2 0.0 slice-start.3
  145.2 11.3 %multiply_convert_fusion.4 = (bf16[256,1792]{1,0:T(8,128)(2,1)S(1)}, f32[256,1792]{1,0:T(8,128)}) fusion(f32[256,1792]{1,0:T(8,128)S(1)} %fusion.10, bf16[1,4096,1792]{2,1,0:T(8,128)(2,1)} %param.18, bf16[512,8,2,128]{3,2,1,0:T(2,128)(2,1)S(1)} %bitcast.102), kind=kOutput, calls=%fused_computation.37 | convolution fusion | flops 3760848896 | bytes 21364736 | tf_op jit(solution)/shard_map/dot_general | solution.py:54
  156.6 5.5 fusion.2
  162.1 0.0 all-reduce.3.cloned.1.call-update
  162.1 0.2 reduce-scatter.2.cloned.1.call-start
  162.3 0.5 copy-done.9
  162.8 0.0 copy-done.10
  162.9 0.8 copy-done.3
  163.7 4.1 copy.30
  167.8 149.2 %all-reduce.3.cloned.1.call-done = f32[256,4096]{1,0:T(8,128)} async-done(((f32[256,4096]{1,0:T(8,128)}), f32[256,4096]{1,0:T(8,128)}) %all-reduce.3.cloned.1.call-update) | async-done | bytes 4194320 | tf_op jit(solution)/shard_map/psum | solution.py:63
  317.1 4.1 multiply_reduce_fusion.1
  321.2 0.5 copy-done.1
  321.7 1.3 copy-done.4
  323.0 3.0 multiply_reduce_fusion
  325.9 0.1 bitcast_reduce_fusion
  326.1 0.1 multiply_reduce_fusion.7
  326.2 0.9 negate_multiply_fusion
  327.0 0.1 multiply_reduce_fusion.6
  327.1 0.7 fusion.33
  327.8 1.3 compare_select_fusion.1
  329.2 2.9 subtract_multiply_fusion
  332.1 12.5 %multiply_convert_fusion.2 = (bf16[256,1792]{1,0:T(8,128)(2,1)}, bf16[256,1792]{1,0:T(8,128)(2,1)}) fusion(f32[256,1792]{1,0:T(8,128)S(1)} %copy-done.6, f32[256,1792]{1,0:T(8,128)} %get-tuple-element.40, bf16[1,1792,4096]{2,1,0:T(8,128)(2,1)} %param.19, f32[256,4096]{1,0:T(8,128)} %subtract_multiply_fusion), kind=kOutput, calls=%fused_computation.35 | convolution fusion | flops 3765108736 | bytes 24379392 | tf_op jit(solution)/shard_map/dot_general | solution.py:25
  344.6 11.5 %fusion.4 = f32[256,4096]{1,0:T(8,128)} fusion(bf16[256,1792]{1,0:T(8,128)(2,1)} %get-tuple-element.27, bf16[1,4096,1792]{2,1,0:T(8,128)(2,1)} %param.18), kind=kOutput, calls=%fused_computation.7 | convolution fusion | flops 3758096384 | bytes 19791872 | tf_op jit(solution)/shard_map/dot_general | solution.py:25
  356.1 17.0 %fusion.15 = f32[256,4096]{1,0:T(8,128)} fusion(f32[256,4096]{1,0:T(8,128)} %fusion.4, bf16[256,1792]{1,0:T(8,128)(2,1)S(1)} %copy-done.7, bf16[1,4096,1792]{2,1,0:T(8,128)(2,1)} %param.17), kind=kOutput, calls=%fused_computation.18 | convolution fusion | flops 3759144960 | bytes 23986176 | tf_op jit(solution)/shard_map/dot_general | solution.py:25
  373.1 0.0 copy-start.12
  373.1 0.0 reduce-scatter.2.cloned.1.call-update
  373.2 0.6 copy-done.12
  373.8 87.0 %reduce-scatter.2.cloned.1.call-done = f32[256,512]{1,0:T(8,128)} async-done(((f32[256,4096]{1,0:T(8,128)}), f32[256,512]{1,0:T(8,128)}) %reduce-scatter.2.cloned.1.call-update) | async-done | bytes 524304 | tf_op jit(solution)/shard_map/reduce_scatter | solution.py:88
  460.8 2.0 multiply_reduce_fusion.3
  462.8 20.1 %psum.22 = f32[256]{0:T(256)S(1)} all-reduce(f32[256]{0:T(256)S(1)} %get-tuple-element.20), channel_id=1, replica_groups=mesh['groups'=2,'member'=2,'fsdp'=8] {'fsdp'}, use_global_device_ids=true, to_apply=%region_13.14 | all-reduce | flops 256 | bytes 2048 | tf_op jit(solution)/shard_map/psum | solution.py:91
  482.9 1.5 add_convert_fusion
  484.4 0.2 copy.31
  484.6 1.5 broadcast_select_fusion.1
  486.1 3.6 all-to-all-start.1
  489.7 0.0 all-reduce.5.cloned.1.call-start
  489.8 12.0 %fusion.12 = bf16[1,4096,1792]{2,1,0:T(8,128)(2,1)} fusion(bf16[256,1792]{1,0:T(8,128)(2,1)} %get-tuple-element.28, f32[256,4096]{1,0:T(8,128)} %get-tuple-element.26, f32[4096]{0:T(1024)S(1)} %bitcast.108), kind=kOutput, calls=%fused_computation.15 | convolution fusion | flops 3767533568 | bytes 19808256 | tf_op jit(solution)/shard_map/dot_general | solution.py:25
  501.8 33.1 %all-to-all-done.1 = bf16[8,2,128,512]{2,3,1,0:T(8,128)(2,1)S(1)} async-done(((bf16[8,2,128,512]{2,3,1,0:T(8,128)(2,1)}), bf16[8,2,128,512]{2,3,1,0:T(8,128)(2,1)S(1)}, u32[]{:S(2)}, u32[]{:S(2)}) %all-to-all-start.1) | async-done | bytes 2097184 | tf_op jit(solution)/shard_map/all_to_all | solution.py:102
  534.9 1.5 copy.32
  536.3 5.0 copy.33
  541.4 2.3 fusion.26
  543.7 2.1 copy.49
  545.8 0.0 all-reduce.5.cloned.1.call-update
  545.8 0.0 copy-start
  545.8 9.9 %fusion.14 = bf16[1,1792,4096]{2,1,0:T(8,128)(2,1)} fusion(bf16[256,1792]{1,0:T(8,128)(2,1)S(1)} %get-tuple-element.39, f32[256,4096]{1,0:T(8,128)} %subtract_multiply_fusion), kind=kOutput, calls=%fused_computation.17 | convolution fusion | flops 3766484992 | bytes 19791872 | tf_op jit(solution)/shard_map/dot_general | solution.py:25
  555.8 1.2 multiply_reduce_fusion.5
  556.9 1.3 dynamic-slice_multiply_fusion
  558.2 8.8 %fusion.13 = bf16[1,4096,1792]{2,1,0:T(8,128)(2,1)} fusion(bf16[256,1792]{1,0:T(8,128)(2,1)} %get-tuple-element.27, f32[256,4096]{1,0:T(8,128)S(1)} %copy-done, f32[4096]{0:T(1024)S(1)} %bitcast.109), kind=kOutput, calls=%fused_computation.16 | convolution fusion | flops 3767533568 | bytes 19808256 | tf_op jit(solution)/shard_map/dot_general | solution.py:25
  567.0 2.3 copy.52
  (35 shorter events, 0.1 us)
Async XLA Ops:
  7.2 111.6 %all-gather.2.cloned.1.call-start = ((), (), s32[]{:S(2)}) async-start(), calls=%async_computation.3 | async-start | bytes 2359296 | tf_op jit(solution)/shard_map/all_gather | solution.py:48
  11.8 112.4 %copy-start.8 = (f32[1,4096]{1,0:T(1,128)S(1)}, f32[1,4096]{1,0:T(1,128)}, u32[]{:S(2)}) copy-start(f32[1,4096]{1,0:T(1,128)} %param.14) | copy-start | bytes 49156
  70.3 246.7 %all-reduce.3.cloned.1.call-start = ((), (), s32[]{:S(2)}) async-start(), calls=%async_computation.4 | async-start | bytes 8388608 | tf_op jit(solution)/shard_map/psum | solution.py:63
  137.1 19.5 %slice-start = ((s8[14680064]{0:T(1024)(128)(4,1)}), s8[4194304]{0:T(1024)(128)(4,1)S(1)}, s32[]{:S(2)}) async-start(s8[14680064]{0:T(1024)(128)(4,1)} %bitcast.120), calls=%async_computation.7 | async-start | bytes 8388608
  137.1 19.5 %slice-start.1 = ((s8[14680064]{0:T(1024)(128)(4,1)}), s8[4194304]{0:T(1024)(128)(4,1)S(1)}, s32[]{:S(2)}) async-start(s8[14680064]{0:T(1024)(128)(4,1)} %bitcast.120), calls=%async_computation.8 | async-start | bytes 8388608
  145.2 11.4 %copy-start.5 = (f32[256,1792]{1,0:T(8,128)}, f32[256,1792]{1,0:T(8,128)S(1)}, u32[]{:S(2)}) copy-start(f32[256,1792]{1,0:T(8,128)S(1)} %fusion.10) | copy-start | bytes 5505028
  145.2 11.4 %slice-start.2 = ((s8[14680064]{0:T(1024)(128)(4,1)}), s8[4194304]{0:T(1024)(128)(4,1)S(1)}, s32[]{:S(2)}) async-start(s8[14680064]{0:T(1024)(128)(4,1)} %bitcast.120), calls=%async_computation.9 | async-start | bytes 8388608
  145.2 11.4 %slice-start.3 = ((s8[14680064]{0:T(1024)(128)(4,1)}), s8[2097152]{0:T(1024)(128)(4,1)S(1)}, s32[]{:S(2)}) async-start(s8[14680064]{0:T(1024)(128)(4,1)} %bitcast.120), calls=%async_computation.10 | async-start | bytes 4194304
  162.1 0.7 copy-start.9
  162.1 0.7 copy-start.10
  162.1 0.8 copy-start.11
  162.1 1.6 copy-start.3
  162.1 298.7 %reduce-scatter.2.cloned.1.call-start = ((), (), s32[]{:S(2)}) async-start(), calls=%async_computation.5 | async-start | bytes 4718592 | tf_op jit(solution)/shard_map/reduce_scatter | solution.py:88
  317.1 4.6 copy-start.1
  317.1 5.9 %copy-start.4 = (f32[256,4096]{1,0:T(8,128)S(1)}, f32[256,4096]{1,0:T(8,128)}, u32[]{:S(2)}) copy-start(f32[256,4096]{1,0:T(8,128)} %all-reduce.3.cloned.1.call-done) | copy-start | bytes 12582916
  325.9 6.1 %copy-start.2 = (f32[256,4096]{1,0:T(8,128)}, f32[256,4096]{1,0:T(8,128)S(1)}, u32[]{:S(2)}) copy-start(f32[256,4096]{1,0:T(8,128)S(1)} %get-tuple-element.25) | copy-start | bytes 12582916
  329.2 2.9 copy-start.6
  344.6 11.5 %copy-start.7 = (bf16[256,1792]{1,0:T(8,128)(2,1)S(1)}, bf16[256,1792]{1,0:T(8,128)(2,1)}, u32[]{:S(2)}) copy-start(bf16[256,1792]{1,0:T(8,128)(2,1)} %get-tuple-element.28) | copy-start | bytes 2752516
  373.1 0.7 copy-start.12
  486.1 48.7 %all-to-all-start.1 = ((bf16[8,2,128,512]{2,3,1,0:T(8,128)(2,1)}), bf16[8,2,128,512]{2,3,1,0:T(8,128)(2,1)S(1)}, u32[]{:S(2)}, u32[]{:S(2)}) async-start(bf16[8,2,128,512]{2,3,1,0:T(8,128)(2,1)} %broadcast_select_fusion.1), calls=%async_computation.2 | async-start | bytes 4194304 | tf_op jit(solution)/shard_map/all_to_all | solution.py:102
  489.7 77.3 %all-reduce.5.cloned.1.call-start = ((), (), s32[]{:S(2)}) async-start(), calls=%async_computation.6 | async-start | bytes 2097152 | tf_op jit(solution)/shard_map/psum | solution.py:110
  545.8 12.4 %copy-start = (f32[256,4096]{1,0:T(8,128)S(1)}, f32[256,4096]{1,0:T(8,128)}, u32[]{:S(2)}) copy-start(f32[256,4096]{1,0:T(8,128)} %get-tuple-element.26) | copy-start | bytes 12582916
Sparse Core Ops, SparseCore 0:
  70.5 48.3 all-gather.1
  162.2 154.7 all-reduce.2
  373.3 87.4 reduce-scatter.1
  546.0 18.4 all-reduce.4
where the time goes:
time: 580 us; the launch traced here: 576 us
  waiting for transfers between devices  317 us (55%)
  matrix products  98.9 us (17%)
  blocking collectives  75.4 us (13%)
  other arithmetic  44.3 us (8%)
  local copies, waits for them, and re-layouts  21.3 us (4%)
  between operations  14.3 us (2%)
    psum x1, waiting for transfers between devices, body(): out_total = lax.psum(out_part, 'fsdp')  149 us
    reduce_scatter x1, waiting for transfers between devices, body(): lax.psum_scatter(dscaled_part, 'fsdp', scatter_dimension=1, tiled=True)  87 us
    dot_general x6, matrix products, contract(): lax.dot_general(left, right, (((left_dim,), (right_dim,)), ((), ())), pre...  71.7 us
    all_to_all x1, blocking collectives, body(): lax.all_to_all(outgoing[None], 'fsdp', split_axis=3, concat_axis=0, tiled...  55.3 us
    all_gather x1, waiting for transfers between devices, body(): gathered = lax.all_gather(bands, 'fsdp', axis=2, tiled=True)  48 us
    all_to_all x1, waiting for transfers between devices, body(): lax.all_to_all(outgoing_back, 'fsdp', split_axis=0, concat_axis=3, tiled=...  33.1 us
    psum x1, blocking collectives, body(): lax.psum(jnp.sum(dnormed_share * normed_in_share, axis=1), 'fsdp')  20.1 us
    convert_element_type x1, other arithmetic, body(): scaled_in = (normed_in * ffn_gain[0][None, :]).astype(jnp.bfloat16)  12.9 us
  transfers between devices with their start and end apart: 5, of which 4 were waited for; matrix products, arithmetic and copies ran while one was open for 6% of the time, Pallas kernels for 0%

commit v1 on v0

--- a/solution.py
+++ b/solution.py
@@ -5,6 +5,15 @@
 
 eps = 1e-05
 loss_scale = 256.0
+
+
+def doubling_sum(x, name):
+    count = lax.axis_size(name)
+    total, reach = (x, 1)
+    while reach < count:
+        total = total + lax.ppermute(total, name, [(i, i ^ reach) for i in range(count)])
+        reach = 2 * reach
+    return total
 
 
 def pair_terms(scores, pair_rows, entries, block_len):
@@ -60,7 +69,7 @@
     head_share = lax.dynamic_slice_in_dim(score_head[0], start, columns, 0)
     ffn_share = lax.dynamic_slice_in_dim(ffn_gain[0], start, columns, 0)
     normed_in_share = lax.dynamic_slice_in_dim(normed_in, start, columns, 1)
-    out_total = lax.psum(out_part, "fsdp")
+    out_total = doubling_sum(out_part, "fsdp")
     summed = inputs + out_total
     inverse_out = lax.rsqrt(jnp.mean(summed * summed, axis=1, keepdims=True) + eps)
     normed_out = summed * inverse_out

time: 580 us -> 798 us (1.38)
  waiting for transfers between devices: 317 us -> 523 us
  other arithmetic: 44.3 us -> 52.7 us
    ppermute x0 -> x3, waiting for transfers between devices: none -> 353 us  [doubling_sum(): lax.ppermute(total, name, [(i, i ^ reach) for i in range(count)])]
    psum x1 -> x0, waiting for transfers between devices: 149 us -> none  [body(): out_total = lax.psum(out_part, 'fsdp')]
  transfers between devices with their start and end apart: 5 -> 7, of which waited for: 4 -> 6; matrix products, arithmetic and copies ran while one was open for 6% -> 5% of each run, Pallas kernels for 0% -> 0%
where the time goes in v1:
time: 798 us; the launch traced here: 791 us
  waiting for transfers between devices  523 us (66%)
  matrix products  97.8 us (12%)
  blocking collectives  75.4 us (9%)
  other arithmetic  52.7 us (7%)
  local copies, waits for them, and re-layouts  18.9 us (2%)
  between operations  14.3 us (2%)
  starting transfers between devices  8.94 us (1%)
    ppermute x3, waiting for transfers between devices, doubling_sum(): lax.ppermute(total, name, [(i, i ^ reach) for i in range(count)])  353 us
    reduce_scatter x1, waiting for transfers between devices, body(): lax.psum_scatter(dscaled_part, 'fsdp', scatter_dimension=1, tiled=True)  88.2 us
    dot_general x6, matrix products, contract(): lax.dot_general(left, right, (((left_dim,), (right_dim,)), ((), ())), pre...  71.7 us
    all_to_all x1, blocking collectives, body(): lax.all_to_all(outgoing[None], 'fsdp', split_axis=3, concat_axis=0, tiled...  55.3 us
    all_gather x1, waiting for transfers between devices, body(): gathered = lax.all_gather(bands, 'fsdp', axis=2, tiled=True)  48.4 us
    all_to_all x1, waiting for transfers between devices, body(): lax.all_to_all(outgoing_back, 'fsdp', split_axis=0, concat_axis=3, tiled=...  33.1 us
    psum x1, blocking collectives, body(): lax.psum(jnp.sum(dnormed_share * normed_in_share, axis=1), 'fsdp')  20.1 us
  transfers between devices with their start and end apart: 7, of which 6 were waited for; matrix products, arithmetic and copies ran while one was open for 5% of the time, Pallas kernels for 0%

profile of v1, /device:TPU:0, one launch (start us, length us, event | category | flops | bytes accessed | tf_op | source)
XLA Modules:
  0.0 791.0 jit_solution(567537601005845803)
XLA Ops:
  7.2 0.0 all-gather.2.cloned.1.call-start
  7.2 1.6 copy.29
  8.8 0.7 broadcast_compare_fusion
  9.5 2.3 broadcast_select_fusion
  11.8 0.0 copy-start.7
  11.8 55.3 %all_to_all.27 = bf16[1,2,128,4096]{2,1,0,3:T(2,128)(2,1)S(1)} all-to-all(bf16[1,2,128,4096]{2,1,0,3:T(2,128)(2,1)S(1)} %broadcast_select_fusion), channel_id=1, replica_groups=mesh['groups'=2,'member'=2,'fsdp'=8] {'fsdp'}, dimensions={3} | all-to-all | bytes 4194304 | tf_op jit(solution)/shard_map/all_to_all | solution.py:55
  67.1 3.2 reduce_sum.104
  70.3 0.0 all-gather.2.cloned.1.call-update
  70.3 0.0 reduce-scatter.2.cloned.1.call-start
  70.4 48.4 %all-gather.2.cloned.1.call-done = bf16[2,128,4096]{1,0,2:T(2,128)(2,1)} async-done(((bf16[2,128,512]{1,0,2:T(2,128)(2,1)}), bf16[2,128,4096]{1,0,2:T(2,128)(2,1)}) %all-gather.2.cloned.1.call-update) | async-done | bytes 2097168 | tf_op jit(solution)/shard_map/all_gather | solution.py:57
  118.8 5.4 multiply_reduce_fusion.2
  124.2 12.9 %multiply_convert_fusion.1 = bf16[2,128,4096]{1,0,2:T(2,128)(2,1)S(1)} fusion(f32[4096]{0:T(1024)S(1)} %bitcast.107, bf16[2,128,4096]{1,0,2:T(2,128)(2,1)} %all-gather.2.cloned.1.call-done, f32[2,128]{1,0:T(2,128)S(1)} %get-tuple-element.32), kind=kLoop, calls=%fused_computation.25 | loop fusion | flops 4194304 | bytes 4211712 | tf_op jit(solution)/shard_map/convert_element_type | solution.py:61
  137.1 0.0 slice-start
  137.1 8.4 %fusion.10 = f32[256,1792]{1,0:T(8,128)S(1)} fusion(bf16[1,4096,1792]{2,1,0:T(8,128)(2,1)} %param.17, bf16[512,8,2,128]{3,2,1,0:T(2,128)(2,1)S(1)} %bitcast.101), kind=kOutput, calls=%fused_computation.13 | convolution fusion | flops 3758096384 | bytes 18612224 | tf_op jit(solution)/shard_map/dot_general | solution.py:62
  145.5 0.0 slice-start.2
  145.5 11.3 %multiply_convert_fusion.4 = (bf16[256,1792]{1,0:T(8,128)(2,1)S(1)}, f32[256,1792]{1,0:T(8,128)}) fusion(f32[256,1792]{1,0:T(8,128)S(1)} %fusion.10, bf16[1,4096,1792]{2,1,0:T(8,128)(2,1)} %param.18, bf16[512,8,2,128]{3,2,1,0:T(2,128)(2,1)S(1)} %bitcast.102), kind=kOutput, calls=%fused_computation.37 | convolution fusion | flops 3760848896 | bytes 21364736 | tf_op jit(solution)/shard_map/dot_general | solution.py:63
  156.9 4.1 fusion.2
  161.0 0.6 collective-permute-start
  161.6 90.6 %collective-permute-done = f32[256,4096]{1,0:T(8,128)S(1)} collective-permute-done((f32[256,4096]{1,0:T(8,128)S(1)}, f32[256,4096]{1,0:T(8,128)S(1)}, u32[]{:S(2)}, u32[]{:S(2)}) %collective-permute-start) | collective-permute-done | bytes 4194336 | tf_op jit(solution)/shard_map/ppermute | solution.py:14
  252.2 0.6 add.139
  252.9 0.0 copy-start.8
  252.9 0.0 copy-start.9
  252.9 0.0 copy-start.10
  252.9 1.8 collective-permute-start.1
  254.7 88.8 %collective-permute-done.1 = f32[256,4096]{1,0:T(8,128)S(1)} collective-permute-done((f32[256,4096]{1,0:T(8,128)S(1)}, f32[256,4096]{1,0:T(8,128)S(1)}, u32[]{:S(2)}, u32[]{:S(2)}) %collective-permute-start.1) | collective-permute-done | bytes 4194336 | tf_op jit(solution)/shard_map/ppermute | solution.py:14
  343.5 2.5 add.140
  346.0 2.8 collective-permute-start.2
  348.9 4.6 copy.30
  353.5 0.0 copy-start.1
  353.5 173.7 %collective-permute-done.2 = f32[256,4096]{1,0:T(8,128)} collective-permute-done((f32[256,4096]{1,0:T(8,128)}, f32[256,4096]{1,0:T(8,128)}, u32[]{:S(2)}, u32[]{:S(2)}) %collective-permute-start.2) | collective-permute-done | bytes 4194336 | tf_op jit(solution)/shard_map/ppermute | solution.py:14
  527.3 5.3 multiply_reduce_fusion.1
  532.6 7.0 multiply_reduce_fusion
  539.6 0.1 bitcast_reduce_fusion
  539.7 0.1 multiply_reduce_fusion.7
  539.8 0.9 negate_multiply_fusion
  540.7 0.1 multiply_reduce_fusion.6
  540.8 0.7 fusion.33
  541.5 1.3 compare_select_fusion.1
  542.8 2.8 subtract_multiply_fusion
  545.6 12.5 %multiply_convert_fusion.2 = (bf16[256,1792]{1,0:T(8,128)(2,1)}, bf16[256,1792]{1,0:T(8,128)(2,1)}) fusion(f32[256,1792]{1,0:T(8,128)S(1)} %copy-done.5, f32[256,1792]{1,0:T(8,128)} %get-tuple-element.40, bf16[1,1792,4096]{2,1,0:T(8,128)(2,1)} %param.19, f32[256,4096]{1,0:T(8,128)} %subtract_multiply_fusion), kind=kOutput, calls=%fused_computation.35 | convolution fusion | flops 3765108736 | bytes 24379392 | tf_op jit(solution)/shard_map/dot_general | solution.py:34
  558.1 11.5 %fusion.4 = f32[256,4096]{1,0:T(8,128)} fusion(bf16[256,1792]{1,0:T(8,128)(2,1)} %get-tuple-element.27, bf16[1,4096,1792]{2,1,0:T(8,128)(2,1)} %param.18), kind=kOutput, calls=%fused_computation.7 | convolution fusion | flops 3758096384 | bytes 19791872 | tf_op jit(solution)/shard_map/dot_general | solution.py:34
  569.7 17.0 %fusion.15 = f32[256,4096]{1,0:T(8,128)} fusion(f32[256,4096]{1,0:T(8,128)} %fusion.4, bf16[256,1792]{1,0:T(8,128)(2,1)S(1)} %copy-done.6, bf16[1,4096,1792]{2,1,0:T(8,128)(2,1)} %param.17), kind=kOutput, calls=%fused_computation.18 | convolution fusion | flops 3759144960 | bytes 23986176 | tf_op jit(solution)/shard_map/dot_general | solution.py:34
  586.6 0.0 reduce-scatter.2.cloned.1.call-update
  586.7 0.6 copy-done.11
  587.3 88.2 %reduce-scatter.2.cloned.1.call-done = f32[256,512]{1,0:T(8,128)} async-done(((f32[256,4096]{1,0:T(8,128)}), f32[256,512]{1,0:T(8,128)}) %reduce-scatter.2.cloned.1.call-update) | async-done | bytes 524304 | tf_op jit(solution)/shard_map/reduce_scatter | solution.py:97
  675.5 2.0 multiply_reduce_fusion.3
  677.5 20.1 %psum.14 = f32[256]{0:T(256)S(1)} all-reduce(f32[256]{0:T(256)S(1)} %get-tuple-element.20), channel_id=1, replica_groups=mesh['groups'=2,'member'=2,'fsdp'=8] {'fsdp'}, use_global_device_ids=true, to_apply=%region_12.13 | all-reduce | flops 256 | bytes 2048 | tf_op jit(solution)/shard_map/psum | solution.py:100
  697.6 1.5 add_convert_fusion
  699.1 0.2 copy.31
  699.3 1.5 broadcast_select_fusion.1
  700.8 3.6 all-to-all-start.1
  704.5 0.0 all-reduce.2.cloned.1.call-start
  704.5 12.0 %fusion.12 = bf16[1,4096,1792]{2,1,0:T(8,128)(2,1)} fusion(bf16[256,1792]{1,0:T(8,128)(2,1)} %get-tuple-element.28, f32[256,4096]{1,0:T(8,128)} %get-tuple-element.26, f32[4096]{0:T(1024)S(1)} %bitcast.108), kind=kOutput, calls=%fused_computation.15 | convolution fusion | flops 3767533568 | bytes 19808256 | tf_op jit(solution)/shard_map/dot_general | solution.py:34
  716.5 33.1 %all-to-all-done.1 = bf16[8,2,128,512]{2,3,1,0:T(8,128)(2,1)S(1)} async-done(((bf16[8,2,128,512]{2,3,1,0:T(8,128)(2,1)}), bf16[8,2,128,512]{2,3,1,0:T(8,128)(2,1)S(1)}, u32[]{:S(2)}, u32[]{:S(2)}) %all-to-all-start.1) | async-done | bytes 2097184 | tf_op jit(solution)/shard_map/all_to_all | solution.py:111
  749.6 1.5 copy.32
  751.0 5.2 copy.33
  756.3 2.3 fusion.26
  758.6 2.1 copy.49
  760.7 0.0 all-reduce.2.cloned.1.call-update
  760.8 9.9 %fusion.14 = bf16[1,1792,4096]{2,1,0:T(8,128)(2,1)} fusion(bf16[256,1792]{1,0:T(8,128)(2,1)S(1)} %get-tuple-element.39, f32[256,4096]{1,0:T(8,128)} %subtract_multiply_fusion), kind=kOutput, calls=%fused_computation.17 | convolution fusion | flops 3766484992 | bytes 19791872 | tf_op jit(solution)/shard_map/dot_general | solution.py:34
  770.7 1.2 multiply_reduce_fusion.5
  771.9 1.3 dynamic-slice_multiply_fusion
  773.2 8.8 %fusion.13 = bf16[1,4096,1792]{2,1,0:T(8,128)(2,1)} fusion(bf16[256,1792]{1,0:T(8,128)(2,1)} %get-tuple-element.27, f32[256,4096]{1,0:T(8,128)S(1)} %copy-done, f32[4096]{0:T(1024)S(1)} %bitcast.109), kind=kOutput, calls=%fused_computation.16 | convolution fusion | flops 3767533568 | bytes 19808256 | tf_op jit(solution)/shard_map/dot_general | solution.py:34
  781.9 2.3 copy.51
  (38 shorter events, 0.2 us)
Async XLA Ops:
  7.2 111.6 %all-gather.2.cloned.1.call-start = ((), (), s32[]{:S(2)}) async-start(), calls=%async_computation.3 | async-start | bytes 2359296 | tf_op jit(solution)/shard_map/all_gather | solution.py:57
  11.8 112.4 %copy-start.7 = (f32[1,4096]{1,0:T(1,128)S(1)}, f32[1,4096]{1,0:T(1,128)}, u32[]{:S(2)}) copy-start(f32[1,4096]{1,0:T(1,128)} %param.14) | copy-start | bytes 49156
  70.3 605.2 %reduce-scatter.2.cloned.1.call-start = ((), (), s32[]{:S(2)}) async-start(), calls=%async_computation.4 | async-start | bytes 4718592 | tf_op jit(solution)/shard_map/reduce_scatter | solution.py:97
  137.1 19.8 %slice-start = ((s8[14680064]{0:T(1024)(128)(4,1)}), s8[4194304]{0:T(1024)(128)(4,1)S(1)}, s32[]{:S(2)}) async-start(s8[14680064]{0:T(1024)(128)(4,1)} %bitcast.120), calls=%async_computation.6 | async-start | bytes 8388608
  137.1 19.8 %slice-start.1 = ((s8[14680064]{0:T(1024)(128)(4,1)}), s8[4194304]{0:T(1024)(128)(4,1)S(1)}, s32[]{:S(2)}) async-start(s8[14680064]{0:T(1024)(128)(4,1)} %bitcast.120), calls=%async_computation.7 | async-start | bytes 8388608
  145.5 11.4 %copy-start.4 = (f32[256,1792]{1,0:T(8,128)}, f32[256,1792]{1,0:T(8,128)S(1)}, u32[]{:S(2)}) copy-start(f32[256,1792]{1,0:T(8,128)S(1)} %fusion.10) | copy-start | bytes 5505028
  145.5 11.4 %slice-start.2 = ((s8[14680064]{0:T(1024)(128)(4,1)}), s8[4194304]{0:T(1024)(128)(4,1)S(1)}, s32[]{:S(2)}) async-start(s8[14680064]{0:T(1024)(128)(4,1)} %bitcast.120), calls=%async_computation.8 | async-start | bytes 8388608
  145.5 11.4 %slice-start.3 = ((s8[14680064]{0:T(1024)(128)(4,1)}), s8[2097152]{0:T(1024)(128)(4,1)S(1)}, s32[]{:S(2)}) async-start(s8[14680064]{0:T(1024)(128)(4,1)} %bitcast.120), calls=%async_computation.9 | async-start | bytes 4194304
  161.0 91.3 %collective-permute-start = (f32[256,4096]{1,0:T(8,128)S(1)}, f32[256,4096]{1,0:T(8,128)S(1)}, u32[]{:S(2)}, u32[]{:S(2)}) collective-permute-start(f32[256,4096]{1,0:T(8,128)S(1)} %fusion.2), channel_id=1, source_target_pairs={{0,1},{1,0},{2,3},{3,2},{4,5},{5,4},{6,7},{7,6},{8,9},{9,8},{10,11... | collective-permute-start | bytes 12582920 | tf_op jit(solution)/shard_map/ppermute | solution.py:14
  252.9 96.0 %copy-start.8 = (f32[1,4096]{1,0:T(1,128)S(1)}, f32[1,4096]{1,0:T(1,128)}, u32[]{:S(2)}) copy-start(f32[1,4096]{1,0:T(1,128)} %param.15) | copy-start | bytes 49156
  252.9 95.9 %copy-start.9 = (f32[1,4096]{1,0:T(1,128)S(1)}, f32[1,4096]{1,0:T(1,128)}, u32[]{:S(2)}) copy-start(f32[1,4096]{1,0:T(1,128)} %param.16) | copy-start | bytes 49156
  252.9 96.0 %copy-start.10 = (s32[1,4,2]{1,2,0:T(2,128)S(1)}, s32[1,4,2]{1,2,0:T(2,128)}, u32[]{:S(2)}) copy-start(s32[1,4,2]{1,2,0:T(2,128)} %param.13) | copy-start | bytes 100
  252.9 96.0 %copy-start.3 = (bf16[2,128,4096]{1,0,2:T(2,128)(2,1)S(1)}, bf16[2,128,4096]{1,0,2:T(2,128)(2,1)}, u32[]{:S(2)}) copy-start(bf16[2,128,4096]{1,0,2:T(2,128)(2,1)} %all-gather.2.cloned.1.call-done) | copy-start | bytes 6291460
  252.9 90.6 %collective-permute-start.1 = (f32[256,4096]{1,0:T(8,128)S(1)}, f32[256,4096]{1,0:T(8,128)S(1)}, u32[]{:S(2)}, u32[]{:S(2)}) collective-permute-start(f32[256,4096]{1,0:T(8,128)S(1)} %add.139), channel_id=1, source_target_pairs={{0,2},{1,3},{2,0},{3,1},{4,6},{5,7},{6,4},{7,5},{8,10},{9,11},{10,... | collective-permute-start | bytes 12582920 | tf_op jit(solution)/shard_map/ppermute | solution.py:14
  346.0 181.2 %collective-permute-start.2 = (f32[256,4096]{1,0:T(8,128)}, f32[256,4096]{1,0:T(8,128)}, u32[]{:S(2)}, u32[]{:S(2)}) collective-permute-start(f32[256,4096]{1,0:T(8,128)} %add.140), channel_id=1, source_target_pairs={{0,4},{1,5},{2,6},{3,7},{4,0},{5,1},{6,2},{7,3},{8,12},{9,13},{10,... | collective-permute-start | bytes 12582920 | tf_op jit(solution)/shard_map/ppermute | solution.py:14
  353.5 179.0 %copy-start.1 = (f32[2,128,4096]{2,1,0:T(8,128)S(1)}, f32[2,128,4096]{2,1,0:T(8,128)}, u32[]{:S(2)}) copy-start(f32[2,128,4096]{2,1,0:T(8,128)} %copy.30) | copy-start | bytes 12582916
  539.6 6.0 copy-start.2
  542.8 2.8 copy-start.5
  558.1 11.5 %copy-start.6 = (bf16[256,1792]{1,0:T(8,128)(2,1)S(1)}, bf16[256,1792]{1,0:T(8,128)(2,1)}, u32[]{:S(2)}) copy-start(bf16[256,1792]{1,0:T(8,128)(2,1)} %get-tuple-element.28) | copy-start | bytes 2752516
  586.6 0.7 copy-start.11
  700.8 48.7 %all-to-all-start.1 = ((bf16[8,2,128,512]{2,3,1,0:T(8,128)(2,1)}), bf16[8,2,128,512]{2,3,1,0:T(8,128)(2,1)S(1)}, u32[]{:S(2)}, u32[]{:S(2)}) async-start(bf16[8,2,128,512]{2,3,1,0:T(8,128)(2,1)} %broadcast_select_fusion.1), calls=%async_computation.2 | async-start | bytes 4194304 | tf_op jit(solution)/shard_map/all_to_all | solution.py:111
  704.5 77.5 %all-reduce.2.cloned.1.call-start = ((), (), s32[]{:S(2)}) async-start(), calls=%async_computation.5 | async-start | bytes 2097152 | tf_op jit(solution)/shard_map/psum | solution.py:119
  760.8 12.4 %copy-start = (f32[256,4096]{1,0:T(8,128)S(1)}, f32[256,4096]{1,0:T(8,128)}, u32[]{:S(2)}) copy-start(f32[256,4096]{1,0:T(8,128)} %get-tuple-element.26) | copy-start | bytes 12582916
Sparse Core Ops, SparseCore 0:
  70.5 48.3 all-gather.1
  586.8 88.6 reduce-scatter.1
  760.9 18.4 all-reduce.1
